TPU v7x, 32 devices: a whole 2x2x4 slice. The times are simulated.
32 devices in a mesh: dp: 8 (over z, x), tensor: 4 (over y, core).
Axes of the slice: x: 2, y: 2, z: 4, core: 2. Of those that a mesh axis runs over, the one named last changes fastest.
Arguments:
- tokens: bfloat16 [4096, 4096], P(('dp', 'tensor')), may hold values from -6 to 6
- norm_gain: float32 [4096], replicated, may hold values from 0.1 to 1.9
- w_query: bfloat16 [4096, 2048], P(None, 'tensor'), may hold values from -2 to 2
- key_weight: bfloat16 [4096, 512], P(None, 'tensor'), may hold values from -0.09375 to 0.09375
- value_weight: bfloat16 [4096, 512], P(None, 'tensor'), may hold values from -0.09375 to 0.09375
- w_out: bfloat16 [2048, 4096], P('tensor'), may hold values from -0.125 to 0.125
- lengths: int32 [4], replicated, may hold values from 1 to 2560, 4096 in all
Outputs:
- layer_out: bfloat16 [4096, 4096], P(('dp', 'tensor'))
Inputs may be any that keep to these rules, and one draw needn't show every extreme that they name: The lengths sum to 4096, and some document has exactly 2560 tokens.
All inputs are finite; a program needn't handle non-finite values.
Results may differ from a plain program's by a relative error of at most 0.0095.
The roundings to bfloat16 on the way count: a program that leaves them out, or rounds other values in their place, can miss the bound.
Values may be sent and summed in bfloat16 or wider, within the bound.
A program may use at most 128 MiB of HBM per device.

v0:
```python
import jax
import jax.numpy as jnp
from jax import lax
from jax.sharding import PartitionSpec as P

HEAD_SIZE = 128


epsilon = 1e-05
rope_base = 500000.0
masked = -1e30
initial_peak = -1e29


def from_behind(block, axis, distance):
    devices = range(lax.axis_size(axis))
    route = [(i - distance, i) for i in devices if i - distance in devices]
    return lax.ppermute(block, axis, route)


def doc_starts(lengths, positions):
    doc_ends = jnp.cumsum(lengths)
    closed = (doc_ends[None, :] <= positions[:, None]).astype(jnp.int32)
    return jnp.sum(closed * lengths[None, :], axis=1)


def rotate(vectors, offsets):
    half_width = vectors.shape[-1] // 2
    exponent = jnp.arange(half_width, dtype=jnp.float32) * (-2.0 / vectors.shape[-1])
    frequency = rope_base**exponent
    angles = offsets.astype(jnp.float32)[:, None] * frequency[None, :]
    cos_part = jnp.cos(angles)[:, None, :]
    sin_part = jnp.sin(angles)[:, None, :]
    leading = vectors[..., :half_width]
    trailing = vectors[..., half_width:]
    return jnp.concatenate(
        [leading * cos_part - trailing * sin_part, trailing * cos_part + leading * sin_part],
        axis=-1,
    )


def project(tokens, norm_gain, w_query, key_weight, value_weight, positions, starts):
    count = tokens.shape[0]
    wide = tokens.astype(jnp.float32)
    inverse = lax.rsqrt(jnp.mean(wide * wide, axis=1, keepdims=True) + epsilon)
    normed = (wide * inverse * norm_gain[None, :]).astype(jnp.bfloat16)
    offsets = positions - starts
    query_rows = jnp.dot(normed, w_query, preferred_element_type=jnp.float32).reshape(
        count, -1, HEAD_SIZE
    )
    query_rows = rotate(query_rows, offsets).astype(jnp.bfloat16)
    key = jnp.dot(normed, key_weight, preferred_element_type=jnp.float32).reshape(
        count, -1, HEAD_SIZE
    )
    key = rotate(key, offsets).astype(jnp.bfloat16)
    value_rows = jnp.dot(normed, value_weight, preferred_element_type=jnp.float32).astype(
        jnp.bfloat16
    )
    return (query_rows, key.reshape(count, -1), value_rows)


def attend_block(carry, keys, values, first_key, context):
    query_rows, positions, starts = context
    length = keys.shape[0]
    heads = query_rows.shape[1]
    key_pos = first_key + jnp.arange(length, dtype=jnp.int32)
    useful = (first_key + length - 1 >= starts[0]) & (first_key <= positions[-1])
    scale = query_rows.shape[-1] ** (-0.5)

    def compute(state):
        peak, mass, summed = state
        key_view = keys.reshape(length, heads, -1)
        value_view = values.reshape(length, heads, -1)
        scores = (
            jnp.einsum("qkgd,skd->qkgs", query_rows, key_view, preferred_element_type=jnp.float32)
            * scale
        )
        visible = (key_pos[None, :] >= starts[:, None]) & (key_pos[None, :] <= positions[:, None])
        scores = jnp.where(visible[:, None, None, :], scores, masked)
        fresh = jnp.maximum(peak, jnp.max(scores, axis=-1))
        shrink = jnp.exp(peak - fresh)
        probs = jnp.exp(scores - fresh[..., None])
        mass = mass * shrink + jnp.sum(probs, axis=-1)
        update = jnp.einsum(
            "qkgs,skd->qkgd",
            probs.astype(jnp.bfloat16),
            value_view,
            preferred_element_type=jnp.float32,
        )
        summed = summed * shrink[..., None] + update
        return (fresh, mass, summed)

    def unchanged(state):
        return state

    return lax.cond(useful, compute, unchanged, carry)


def fold_keys(carry, pieces, start, context):
    keys, values = pieces
    width = keys.shape[0]
    size = min(width, 1024)
    whole = width // size

    def one_block(index, state):
        offset = (index * size).astype(jnp.int32)
        return attend_block(state, keys, values, start + offset, context)

    carry = lax.fori_loop(0, whole, one_block, carry)
    return carry


def body(tokens, norm_gain, w_query, key_weight, value_weight, w_out, lengths):
    gathered = lax.all_gather(tokens, "tensor", axis=0, tiled=True)
    count = gathered.shape[0]
    first = lax.axis_index("dp") * count
    positions = first + jnp.arange(count, dtype=jnp.int32)
    starts = doc_starts(lengths, positions)
    query_rows, key, value_rows = project(
        gathered, norm_gain, w_query, key_weight, value_weight, positions, starts
    )
    heads = key.shape[1] // HEAD_SIZE
    query_rows = query_rows.reshape(count, heads, -1, HEAD_SIZE)
    group_count = query_rows.shape[2]
    context = (query_rows, positions, starts)
    initial = (
        jnp.full((count, heads, group_count), initial_peak, jnp.float32),
        jnp.zeros((count, heads, group_count), jnp.float32),
        jnp.zeros((count, heads, group_count, HEAD_SIZE), jnp.float32),
    )
    carry = fold_keys(initial, (key, value_rows), first, context)
    paired = jnp.stack([key, value_rows])
    reach = lax.axis_size("dp") // 2 + 1

    def one_step(back, state):
        moving, accum = state
        moving = from_behind(moving, "dp", 1)
        accum = fold_keys(accum, (moving[0], moving[1]), first - back * count, context)
        return (moving, accum)

    paired, carry = lax.fori_loop(1, reach + 1, one_step, (paired, carry))
    peak, mass, summed = carry
    attended = (summed / mass[..., None]).reshape(count, -1).astype(jnp.bfloat16)
    branch = lax.psum_scatter(
        jnp.dot(attended, w_out, preferred_element_type=jnp.float32).astype(jnp.bfloat16),
        "tensor",
        scatter_dimension=0,
        tiled=True,
    ).astype(jnp.float32)
    return (tokens.astype(jnp.float32) + branch).astype(jnp.bfloat16)


def solution(mesh):
    in_specs = (
        P(("dp", "tensor"), None),
        P(),
        P(None, "tensor"),
        P(None, "tensor"),
        P(None, "tensor"),
        P("tensor", None),
        P(),
    )
    out_specs = P(("dp", "tensor"), None)
    return jax.shard_map(body, mesh=mesh, in_specs=in_specs, out_specs=out_specs, check_vma=False)
```

profile of v0, /device:TPU:0, one launch (start us, length us, event | category | flops | bytes accessed | tf_op | source)
XLA Modules:
  0.0 201.6 jit_solution(4432884227593100175)
XLA Ops:
  12.5 1.8 multiply_cosine_fusion
  14.3 31.8 %all-gather.2.cloned.1.call-done = bf16[512,4096]{1,0:T(8,128)(2,1)} async-done(((bf16[128,4096]{1,0:T(8,128)(2,1)}), bf16[512,4096]{1,0:T(8,128)(2,1)}) %all-gather.2.cloned.1.call-update) | async-done | bytes 4194320 | tf_op jit(solution)/shard_map/all_gather | solution.py:114
  46.1 3.2 %fusion.42 = f32[512]{0:T(512)S(1)} fusion(bf16[512,4096]{1,0:T(8,128)(2,1)} %all-gather.2.cloned.1.call-done), kind=kLoop, calls=%fused_computation.47 | loop fusion | flops 6290944 | bytes 4196352 | tf_op jit(solution)/shard_map/reduce_sum | solution.py:45
  49.6 1.6 convolution_bitcast_fusion
  51.8 1.6 convolution_convert_fusion.1
  54.3 5.9 %fusion.55 = f32[512,512]{0,1:T(8,128)S(1)} fusion(bf16[4096,512]{1,0:T(8,128)(2,1)} %param.15, bf16[512,4096]{1,0:T(8,128)(2,1)} %all-gather.2.cloned.1.call-done, f32[4096]{0:T(1024)S(1)} %copy-done.13, f32[512]{0:T(512)S(1)} %add_rsqrt_fusion), kind=kOutput, calls=%fused_computation.79 | convolution fusion | flops 2155872256 | bytes 9455616 | tf_op jit(solution)/shard_map/dot_general | solution.py:48
  61.5 1.4 copy.39
  64.4 5.8 %conditional.2 = ((f32[512,1,4]{0,2,1:T(4,128)S(1)}, f32[512,1,4]{0,2,1:T(4,128)S(1)}, f32[512,1,4,128]{3,0,2,1:T(8,128)})) conditional(s32[]{:T(128)} %convert_element_type.89, (f32[512,1,4]{0,2,1:T(4,128)S(1)}, f32[512,1,4]{0,2,1:T(4,128)S(1)}, f32[512,1,4,128]{3,0,2,1:T(8,128)}) %tuple.55, (s32[512]{0:T(512)}, s32[512]{0:T(512)}, ...), branch_computations={%region_3.4_spmd, %region_4.7_spmd} | conditional | flops 549722112 | bytes 25563252 | solution.py:96
  67.6 1.6 fusion.10
  70.2 56.5 %while.45 = (s32[]{:T(128)}, bf16[2,512,128]{2,1,0:T(8,128)(2,1)S(1)}, f32[512,1,4]{0,2,1:T(4,128)S(1)}, f32[512,1,4]{0,2,1:T(4,128)S(1)}, f32[512,1,4,128]{3,0,...) while((s32[]{:T(128)}, ...), condition=%wide.region_12.13_spmd, body=%wide.region_7.12_spmd.sunk | while | flops 549722624 | bytes 26620328 | solution.py:141
  70.2 3.4 %collective-permute-start = (bf16[2,512,128]{2,1,0:T(8,128)(2,1)S(1)}, bf16[2,512,128]{2,1,0:T(8,128)(2,1)S(1)}, u32[]{:S(2)}, u32[]{:S(2)}) collective-permute-start(bf16[2,512,128]{2,1,0:T(8,128)(2,1)S(1)} %get-tuple-element.655), channel_id=1, source_target_pairs={{0,4},{4,8},{8,12},{12,16},{16,20},{20,24},{24,28},{1,5},{5,9},{9,... | collective-permute-start | bytes 786440 | tf_op jit(solution)/shard_map/while/body/eval_jaxpr/ppermute | solution.py:18
  74.8 1.3 slice.95
  77.2 2.3 %collective-permute-done = bf16[2,512,128]{2,1,0:T(8,128)(2,1)S(1)} collective-permute-done((bf16[2,512,128]{2,1,0:T(8,128)(2,1)S(1)}, bf16[2,512,128]{2,1,0:T(8,128)(2,1)S(1)}, u32[]{:S(2)}, u32[]{:S(2)}) %collective-permute-start) | collective-permute-done | bytes 262176 | tf_op jit(solution)/shard_map/while/body/eval_jaxpr/ppermute | solution.py:18
  79.6 9.7 %collective-permute-start = (bf16[2,512,128]{2,1,0:T(8,128)(2,1)S(1)}, bf16[2,512,128]{2,1,0:T(8,128)(2,1)S(1)}, u32[]{:S(2)}, u32[]{:S(2)}) collective-permute-start(bf16[2,512,128]{2,1,0:T(8,128)(2,1)S(1)} %get-tuple-element.655), channel_id=1, source_target_pairs={{0,4},{4,8},{8,12},{12,16},{16,20},{20,24},{24,28},{1,5},{5,9},{9,... | collective-permute-start | bytes 786440 | tf_op jit(solution)/shard_map/while/body/eval_jaxpr/ppermute | solution.py:18
  92.9 1.4 collective-permute-done
  94.4 4.4 %collective-permute-start = (bf16[2,512,128]{2,1,0:T(8,128)(2,1)S(1)}, bf16[2,512,128]{2,1,0:T(8,128)(2,1)S(1)}, u32[]{:S(2)}, u32[]{:S(2)}) collective-permute-start(bf16[2,512,128]{2,1,0:T(8,128)(2,1)S(1)} %get-tuple-element.655), channel_id=1, source_target_pairs={{0,4},{4,8},{8,12},{12,16},{16,20},{20,24},{24,28},{1,5},{5,9},{9,... | collective-permute-start | bytes 786440 | tf_op jit(solution)/shard_map/while/body/eval_jaxpr/ppermute | solution.py:18
  100.0 1.3 slice.95
  103.1 10.5 %collective-permute-start = (bf16[2,512,128]{2,1,0:T(8,128)(2,1)S(1)}, bf16[2,512,128]{2,1,0:T(8,128)(2,1)S(1)}, u32[]{:S(2)}, u32[]{:S(2)}) collective-permute-start(bf16[2,512,128]{2,1,0:T(8,128)(2,1)S(1)} %get-tuple-element.655), channel_id=1, source_target_pairs={{0,4},{4,8},{8,12},{12,16},{16,20},{20,24},{24,28},{1,5},{5,9},{9,... | collective-permute-start | bytes 786440 | tf_op jit(solution)/shard_map/while/body/eval_jaxpr/ppermute | solution.py:18
  117.5 5.3 %collective-permute-start = (bf16[2,512,128]{2,1,0:T(8,128)(2,1)S(1)}, bf16[2,512,128]{2,1,0:T(8,128)(2,1)S(1)}, u32[]{:S(2)}, u32[]{:S(2)}) collective-permute-start(bf16[2,512,128]{2,1,0:T(8,128)(2,1)S(1)} %get-tuple-element.655), channel_id=1, source_target_pairs={{0,4},{4,8},{8,12},{12,16},{16,20},{20,24},{24,28},{1,5},{5,9},{9,... | collective-permute-start | bytes 786440 | tf_op jit(solution)/shard_map/while/body/eval_jaxpr/ppermute | solution.py:18
  124.0 1.3 slice.95
  126.7 1.6 copy.33
  128.4 6.5 %convolution_convert_fusion = bf16[512,4096]{1,0:T(8,128)(2,1)} fusion(bf16[512,512]{0,1:T(8,128)(2,1)S(1)} %bitcast.139, bf16[512,4096]{1,0:T(8,128)(2,1)} %param.18), kind=kOutput, calls=%fused_computation.50 | convolution fusion | flops 2149580800 | bytes 8912896 | tf_op jit(solution)/shard_map/dot_general | solution.py:145
  134.9 57.4 %reduce-scatter.2.cloned.1.call-done = bf16[128,4096]{1,0:T(8,128)(2,1)} async-done(((bf16[512,4096]{1,0:T(8,128)(2,1)}), bf16[128,4096]{1,0:T(8,128)(2,1)}) %reduce-scatter.2.cloned.1.call-update) | async-done | bytes 1048592 | tf_op jit(solution)/shard_map/reduce_scatter | solution.py:144
  192.3 2.4 %add_convert_fusion = bf16[128,4096]{1,0:T(8,128)(2,1)} fusion(bf16[128,4096]{1,0:T(8,128)(2,1)} %reduce-scatter.2.cloned.1.call-done, bf16[128,4096]{1,0:T(8,128)(2,1)S(1)} %copy-done.1), kind=kLoop, calls=%fused_computation.51 | loop fusion | flops 2097152 | bytes 3145728 | tf_op jit(solution)/shard_map/convert_element_type | solution.py:150
  (79 shorter events, 22.5 us)
Async XLA Ops:
  6.5 42.8 %copy-start = (bf16[4096,128]{1,0:T(8,128)(2,1)S(1)}, bf16[4096,128]{1,0:T(8,128)(2,1)}, u32[]{:S(2)}) copy-start(bf16[4096,128]{1,0:T(8,128)(2,1)} %param.16) | copy-start | bytes 3145732
  6.5 42.8 %copy-start.13 = (f32[4096]{0:T(1024)S(1)}, f32[4096]{0:T(1024)}, u32[]{:S(2)}) copy-start(f32[4096]{0:T(1024)} %param.14) | copy-start | bytes 49156
  6.5 39.6 %all-gather.2.cloned.1.call-start = ((), (), s32[]{:S(2)}) async-start(), calls=%async_computation.1 | async-start | bytes 5242880 | tf_op jit(solution)/shard_map/all_gather | solution.py:114
  7.3 185.0 %reduce-scatter.2.cloned.1.call-start = ((), (), s32[]{:S(2)}) async-start(), calls=%async_computation.2 | async-start | bytes 5242880 | tf_op jit(solution)/shard_map/reduce_scatter | solution.py:144
  7.3 43.9 %copy-start.8 = (s32[512]{0:T(512)}, s32[512]{0:T(512)S(1)}, u32[]{:S(2)}) copy-start(s32[512]{0:T(512)S(1)} %iota_add_fusion) | copy-start | bytes 6148
  9.6 2.9 %copy-start.9 = (s32[512]{0:T(512)}, s32[512]{0:T(512)S(1)}, u32[]{:S(2)}) copy-start(s32[512]{0:T(512)S(1)} %select_reduce_fusion) | copy-start | bytes 6148
  46.1 3.4 %copy-start.2 = (bf16[512,4096]{1,0:T(8,128)(2,1)S(1)}, bf16[512,4096]{1,0:T(8,128)(2,1)}, u32[]{:S(2)}) copy-start(bf16[512,4096]{1,0:T(8,128)(2,1)} %all-gather.2.cloned.1.call-done) | copy-start | bytes 12582916
  49.6 2.2 %copy-start.12 = (bf16[4096,128]{1,0:T(8,128)(2,1)S(1)}, bf16[4096,128]{1,0:T(8,128)(2,1)}, u32[]{:S(2)}) copy-start(bf16[4096,128]{1,0:T(8,128)(2,1)} %param.17) | copy-start | bytes 3145732
  53.4 6.8 %copy-start.10 = (bf16[512,128]{0,1:T(8,128)(2,1)}, bf16[512,128]{0,1:T(8,128)(2,1)S(1)}, u32[]{:S(2)}) copy-start(bf16[512,128]{0,1:T(8,128)(2,1)S(1)} %convolution_convert_fusion.1) | copy-start | bytes 393220
  64.4 5.8 %copy-start.7 = (bf16[2,512,128]{2,1,0:T(8,128)(2,1)S(1)}, bf16[2,512,128]{2,1,0:T(8,128)(2,1)}, u32[]{:S(2)}) copy-start(bf16[2,512,128]{2,1,0:T(8,128)(2,1)} %copy.32) | copy-start | bytes 786436
  65.6 1.9 copy-start.3
  65.6 1.9 copy-start.11
  69.2 1.0 copy-start.4
  70.2 9.3 %collective-permute-start = (bf16[2,512,128]{2,1,0:T(8,128)(2,1)S(1)}, bf16[2,512,128]{2,1,0:T(8,128)(2,1)S(1)}, u32[]{:S(2)}, u32[]{:S(2)}) collective-permute-start(bf16[2,512,128]{2,1,0:T(8,128)(2,1)S(1)} %get-tuple-element.655), channel_id=1, source_target_pairs={{0,4},{4,8},{8,12},{12,16},{16,20},{20,24},{24,28},{1,5},{5,9},{9,... | collective-permute-start | bytes 786440 | tf_op jit(solution)/shard_map/while/body/eval_jaxpr/ppermute | solution.py:18
  79.6 14.8 %collective-permute-start = (bf16[2,512,128]{2,1,0:T(8,128)(2,1)S(1)}, bf16[2,512,128]{2,1,0:T(8,128)(2,1)S(1)}, u32[]{:S(2)}, u32[]{:S(2)}) collective-permute-start(bf16[2,512,128]{2,1,0:T(8,128)(2,1)S(1)} %get-tuple-element.655), channel_id=1, source_target_pairs={{0,4},{4,8},{8,12},{12,16},{16,20},{20,24},{24,28},{1,5},{5,9},{9,... | collective-permute-start | bytes 786440 | tf_op jit(solution)/shard_map/while/body/eval_jaxpr/ppermute | solution.py:18
  94.4 8.6 %collective-permute-start = (bf16[2,512,128]{2,1,0:T(8,128)(2,1)S(1)}, bf16[2,512,128]{2,1,0:T(8,128)(2,1)S(1)}, u32[]{:S(2)}, u32[]{:S(2)}) collective-permute-start(bf16[2,512,128]{2,1,0:T(8,128)(2,1)S(1)} %get-tuple-element.655), channel_id=1, source_target_pairs={{0,4},{4,8},{8,12},{12,16},{16,20},{20,24},{24,28},{1,5},{5,9},{9,... | collective-permute-start | bytes 786440 | tf_op jit(solution)/shard_map/while/body/eval_jaxpr/ppermute | solution.py:18
  103.1 14.4 %collective-permute-start = (bf16[2,512,128]{2,1,0:T(8,128)(2,1)S(1)}, bf16[2,512,128]{2,1,0:T(8,128)(2,1)S(1)}, u32[]{:S(2)}, u32[]{:S(2)}) collective-permute-start(bf16[2,512,128]{2,1,0:T(8,128)(2,1)S(1)} %get-tuple-element.655), channel_id=1, source_target_pairs={{0,4},{4,8},{8,12},{12,16},{16,20},{20,24},{24,28},{1,5},{5,9},{9,... | collective-permute-start | bytes 786440 | tf_op jit(solution)/shard_map/while/body/eval_jaxpr/ppermute | solution.py:18
  117.5 9.2 %collective-permute-start = (bf16[2,512,128]{2,1,0:T(8,128)(2,1)S(1)}, bf16[2,512,128]{2,1,0:T(8,128)(2,1)S(1)}, u32[]{:S(2)}, u32[]{:S(2)}) collective-permute-start(bf16[2,512,128]{2,1,0:T(8,128)(2,1)S(1)} %get-tuple-element.655), channel_id=1, source_target_pairs={{0,4},{4,8},{8,12},{12,16},{16,20},{20,24},{24,28},{1,5},{5,9},{9,... | collective-permute-start | bytes 786440 | tf_op jit(solution)/shard_map/while/body/eval_jaxpr/ppermute | solution.py:18
  134.9 57.4 %copy-start.1 = (bf16[128,4096]{1,0:T(8,128)(2,1)S(1)}, bf16[128,4096]{1,0:T(8,128)(2,1)}, u32[]{:S(2)}) copy-start(bf16[128,4096]{1,0:T(8,128)(2,1)} %param.13) | copy-start | bytes 3145732
Sparse Core Ops, SparseCore 0:
  8.9 37.1 all-gather.1
  135.1 57.1 reduce-scatter.1
where the time goes:
time: 205 us; the launch traced here: 202 us
  waiting for transfers between devices  94.5 us (46%)
  starting transfers between devices  33.3 us (16%)
  local copies, waits for them, and re-layouts  20.8 us (10%)
  matrix products  18.3 us (9%)
  between operations  14.9 us (7%)
  other arithmetic  13.2 us (6%)
  loops' own time  6.45 us (3%)
    reduce_scatter x1, waiting for transfers between devices, body(): lax.psum_scatter(jnp.dot(attended, w_out, preferred_element_type=jnp.floa...  57.4 us
    ppermute x5, starting transfers between devices, from_behind(): return lax.ppermute(block, axis, route)  33.3 us
    all_gather x1, waiting for transfers between devices, body(): gathered = lax.all_gather(tokens, 'tensor', axis=0, tiled=True)  31.8 us
    slice x6, local copies, waits for them, and re-layouts, attend_block(): positions[-1]  7.09 us
    dot_general x1, matrix products, body(): jnp.dot(attended, w_out, preferred_element_type=jnp.float32)  6.51 us
    slice x6, local copies, waits for them, and re-layouts, attend_block(): starts[0]  6.39 us
    another operation x1, loops' own time, body(): paired, carry = lax.fori_loop(1, reach + 1, one_step, (paired, carry))  6.17 us
    dot_general x1, matrix products, project(): jnp.dot(normed, w_query, preferred_element_type=jnp.float32)  5.94 us
  transfers between devices with their start and end apart: 7, of which 7 were waited for; matrix products, arithmetic and copies ran while one was open for 9% of the time, Pallas kernels for 0%

commit v1 on v0

v1 whole, which is shorter than its diff:
```python
import functools
import math

import jax
import jax.numpy as jnp
from jax import lax
from jax.experimental import pallas as pl
from jax.experimental.pallas import tpu as pltpu
from jax.sharding import PartitionSpec as P

HEAD_SIZE = 128
MESH = pl.DeviceIdType.MESH

epsilon = 1e-05
rope_base = 500000.0
masked = -1e30
initial_peak = -1e29


def doc_starts(lengths, positions):
    doc_ends = jnp.cumsum(lengths)
    closed = (doc_ends[None, :] <= positions[:, None]).astype(jnp.int32)
    return jnp.sum(closed * lengths[None, :], axis=1)


def flip(index, bits):
    low, high = index % 2, index // 2
    if bits & 1:
        low = 1 - low
    if bits & 2:
        high = 1 - high
    return high * 2 + low


def project_kernel(
    chunks, tokens, gain, cos_ref, sin_ref, wq, wk, wv,
    q_out, kv_out,
    held, normed, weight, raw, own_sem, weight_sem, send1, recv1, send2, recv2, send3, recv3,
):
    me = lax.axis_index("tensor")
    near, far = flip(me, 1), flip(me, 2)
    rows = tokens.shape[0]
    piece = rows // chunks
    heads = q_out.shape[0]
    q_width = wq.shape[1]
    kv_width = wk.shape[1]

    loads = [
        pltpu.make_async_copy(tokens, held.at[0], own_sem),
        pltpu.make_async_copy(wq, weight.at[:, pl.ds(0, q_width)], weight_sem.at[0]),
        pltpu.make_async_copy(wk, weight.at[:, pl.ds(q_width, kv_width)], weight_sem.at[1]),
        pltpu.make_async_copy(wv, weight.at[:, pl.ds(q_width + kv_width, kv_width)], weight_sem.at[2]),
    ]
    for load in loads:
        load.start()

    barrier = pltpu.get_barrier_semaphore()
    for other in (near, far):
        pl.semaphore_signal(barrier, inc=1, device_id={"tensor": other}, device_id_type=MESH)
    pl.semaphore_wait(barrier, 2)

    def remote(src, dst, send, recv, other):
        return pltpu.make_async_remote_copy(
            src_ref=src, dst_ref=dst, send_sem=send, recv_sem=recv,
            device_id={"tensor": other}, device_id_type=MESH,
        )

    cross = [
        remote(
            tokens.at[pl.ds(c * piece, piece), :], held.at[2, pl.ds(c * piece, piece), :],
            send2.at[c], recv2.at[c], far,
        )
        for c in range(chunks)
    ]
    for copy in cross:
        copy.start()
    sideways = remote(tokens, held.at[1], send1, recv1, near)
    sideways.start()

    def project(slot):
        block = flip(me, slot) if slot else me
        first = pl.multiple_of(block * rows, rows)
        wide = held[slot].astype(jnp.float32)
        inverse = lax.rsqrt(jnp.mean(wide * wide, axis=1, keepdims=True) + epsilon)
        normed[...] = (wide * inverse * gain[...]).astype(jnp.bfloat16)

        tile = 256
        @pl.loop(0, weight.shape[1] // tile)
        def _(n):
            columns = pl.ds(pl.multiple_of(n * tile, tile), tile)
            raw[:, columns] = jnp.dot(normed[...], weight[:, columns], preferred_element_type=jnp.float32)

        cos = cos_ref[pl.ds(first, rows), :]
        sin = sin_ref[pl.ds(first, rows), :]

        def rotated(index):
            part = raw[:, index * HEAD_SIZE:(index + 1) * HEAD_SIZE]
            return (part * cos + pltpu.roll(part, HEAD_SIZE // 2, 1) * sin).astype(jnp.bfloat16)

        for h in range(heads):
            q_out[h, pl.ds(first, rows), :] = rotated(h)
        kv_out[0, pl.ds(first, rows), :] = rotated(heads)
        kv_out[1, pl.ds(first, rows), :] = raw[:, (heads + 1) * HEAD_SIZE:].astype(jnp.bfloat16)

    for load in loads:
        load.wait()
    project(0)
    sideways.wait_recv()
    project(1)
    relays = []
    for c in range(chunks):
        cross[c].wait_recv()
        part = held.at[2, pl.ds(c * piece, piece), :]
        relay = remote(part, held.at[3, pl.ds(c * piece, piece), :], send3.at[c], recv3.at[c], near)
        relay.start()
        relays.append(relay)
    project(2)
    for relay in relays:
        relay.wait_recv()
    project(3)
    sideways.wait_send()
    for copy in cross + relays:
        copy.wait_send()


def project_call(tokens, gain, cos, sin, wq, wk, wv, tensor):
    rows, width = tokens.shape
    count = rows * tensor
    heads = wq.shape[1] // HEAD_SIZE
    total = wq.shape[1] + wk.shape[1] + wv.shape[1]
    chunks = 4
    any_spec = pl.BlockSpec(memory_space=pl.ANY)
    vmem = pl.BlockSpec(memory_space=pltpu.VMEM)
    return pl.pallas_call(
        functools.partial(project_kernel, chunks),
        out_shape=(
            jax.ShapeDtypeStruct((heads, count, HEAD_SIZE), jnp.bfloat16),
            jax.ShapeDtypeStruct((2, count, HEAD_SIZE), jnp.bfloat16),
        ),
        in_specs=[any_spec, vmem, vmem, vmem, any_spec, any_spec, any_spec],
        out_specs=(vmem, vmem),
        scratch_shapes=[
            pltpu.VMEM((4, rows, width), jnp.bfloat16),
            pltpu.VMEM((rows, width), jnp.bfloat16),
            pltpu.VMEM((width, total), jnp.bfloat16),
            pltpu.VMEM((rows, total), jnp.float32),
            pltpu.SemaphoreType.DMA,
            pltpu.SemaphoreType.DMA((3,)),
            pltpu.SemaphoreType.DMA,
            pltpu.SemaphoreType.DMA,
            pltpu.SemaphoreType.DMA((chunks,)),
            pltpu.SemaphoreType.DMA((chunks,)),
            pltpu.SemaphoreType.DMA((chunks,)),
            pltpu.SemaphoreType.DMA((chunks,)),
        ],
        compiler_params=pltpu.CompilerParams(
            collective_id=0, has_side_effects=True, vmem_limit_bytes=60 * 2**20
        ),
        name="gather_project",
    )(tokens, gain, cos, sin, wq, wk, wv)


def attend_kernel(
    dp, reach, chunks, q_ref, kv_ref, starts, tokens, w_out,
    out_ref,
    ring, peak, mass, summed, attended, weight, part_a, part_b, part_c, got_a, got_b, got_c, mine,
    load_sem, z_send, x_send, ring_recv, send_a, recv_a, send_b, recv_b, send_c, recv_c,
):
    me = lax.axis_index("tensor")
    here = lax.axis_index("dp")
    odd = here % 2
    heads, count, _ = q_ref.shape
    rows = count // 4
    near, far = flip(me, 1), flip(me, 2)
    partner = here + 1 - 2 * odd

    loads = [
        pltpu.make_async_copy(w_out, weight, load_sem.at[0]),
        pltpu.make_async_copy(tokens, mine, load_sem.at[1]),
    ]
    for load in loads:
        load.start()

    barrier = pltpu.get_barrier_semaphore()
    for other in (near, far):
        pl.semaphore_signal(barrier, inc=1, device_id={"tensor": other}, device_id_type=MESH)
    pl.semaphore_signal(barrier, inc=1, device_id={"dp": partner}, device_id_type=MESH)

    for other in ((here + 2) % dp, (here + dp - 2) % dp):
        pl.semaphore_signal(barrier, inc=1, device_id={"dp": other}, device_id_type=MESH)
    pl.semaphore_wait(barrier, 5)

    last_even = reach + 1 if reach % 2 else reach

    def along(src, j):
        return pltpu.make_async_remote_copy(
            src_ref=src, dst_ref=ring.at[j + 2], send_sem=z_send.at[j], recv_sem=ring_recv.at[j + 2],
            device_id={"dp": here + 2}, device_id_type=MESH,
        )

    def across(src, j):
        target = j + 1 - 2 * odd
        return pltpu.make_async_remote_copy(
            src_ref=src, dst_ref=ring.at[target], send_sem=x_send.at[j], recv_sem=ring_recv.at[target],
            device_id={"dp": partner}, device_id_type=MESH,
        )

    def goes_along(j):
        return (here + 2 < dp) & (j + 2 <= reach + odd) & (here >= j)

    def goes_across(j):
        target = j + 1 - 2 * odd
        return (target >= 1) & (target <= reach) & (here >= j)

    def forward(src, j):
        @pl.when(goes_along(j))
        def _():
            along(src, j).start()

        @pl.when(goes_across(j))
        def _():
            across(src, j).start()

    def settle(j):
        @pl.when(goes_along(j))
        def _():
            along(kv_ref, j).wait_send()

        @pl.when(goes_across(j))
        def _():
            across(kv_ref, j).wait_send()

    def arrive(j):
        pltpu.make_async_remote_copy(
            src_ref=kv_ref, dst_ref=ring.at[j], send_sem=z_send.at[j], recv_sem=ring_recv.at[j],
            device_id={"dp": partner}, device_id_type=MESH,
        ).wait_recv()

    forward(kv_ref, 0)

    scale = HEAD_SIZE ** (-0.5) * math.log2(math.e)
    block = 256
    tiles = heads * count // block
    per_head = count // block

    def scores_of(h, row, keys):
        scores = lax.dot_general(
            q_ref[h, pl.ds(row, block), :], keys, (((1,), (1,)), ((), ())),
            preferred_element_type=jnp.float32,
        )
        return scores * scale

    @pl.loop(0, tiles)
    def _(i):
        h, row = i // per_head, pl.multiple_of(i % per_head * block, block)
        scores = scores_of(h, row, kv_ref[0])
        key_pos = lax.broadcasted_iota(jnp.int32, (block, count), 1)
        query_pos = row + lax.broadcasted_iota(jnp.int32, (block, 1), 0)
        begin = starts[pl.ds(row, block), :] - here * count
        scores = jnp.where((key_pos >= begin) & (key_pos <= query_pos), scores, masked)
        top = jnp.max(scores, axis=1, keepdims=True)
        probs = jnp.exp2(scores - top)
        peak[h, pl.ds(row, block), :] = top
        mass[h, pl.ds(row, block), :] = jnp.sum(probs, axis=1, keepdims=True)
        summed[h, pl.ds(row, block), :] = jnp.dot(
            probs.astype(jnp.bfloat16), kv_ref[1], preferred_element_type=jnp.float32
        )

    def fold(j):
        @pl.loop(0, tiles)
        def _(i):
            h, row = i // per_head, pl.multiple_of(i % per_head * block, block)
            scores = scores_of(h, row, ring[j, 0])
            key_pos = lax.broadcasted_iota(jnp.int32, (block, count), 1)
            begin = starts[pl.ds(row, block), :] - (here - j) * count
            scores = jnp.where(key_pos >= begin, scores, masked)
            old = peak[h, pl.ds(row, block), :]
            top = jnp.maximum(old, jnp.max(scores, axis=1, keepdims=True))
            shrink = jnp.exp2(old - top)
            probs = jnp.exp2(scores - top)
            peak[h, pl.ds(row, block), :] = top
            mass[h, pl.ds(row, block), :] = mass[h, pl.ds(row, block), :] * shrink + jnp.sum(
                probs, axis=1, keepdims=True
            )
            summed[h, pl.ds(row, block), :] = summed[h, pl.ds(row, block), :] * shrink + jnp.dot(
                probs.astype(jnp.bfloat16), ring[j, 1], preferred_element_type=jnp.float32
            )

    @pl.loop(0, last_even // 2)
    def _(step):
        even = 2 * step + 2

        @pl.when((here >= even) & (even <= reach + odd))
        def _():
            arrive(even)
            forward(ring.at[even], even)

        @pl.when((here >= even) & (even <= reach))
        def _():
            fold(even)

        @pl.when(here >= even - 1)
        def _():
            arrive(even - 1)
            fold(even - 1)

    for h in range(heads):
        attended[:, h * HEAD_SIZE:(h + 1) * HEAD_SIZE] = (summed[h] / mass[h]).astype(jnp.bfloat16)

    @pl.loop(0, last_even // 2 + 1)
    def _(step):
        @pl.when(2 * step <= reach + odd)
        def _():
            settle(2 * step)

    for load in loads:
        load.wait()
    wide = weight.shape[1] // chunks

    def share(block_of, c):
        first = pl.multiple_of(block_of * rows, rows)
        columns = pl.ds(pl.multiple_of(c * wide, wide), wide)
        return jnp.dot(attended[pl.ds(first, rows), :], weight[:, columns], preferred_element_type=jnp.float32)

    def hand(src, dst, send, recv, c, other):
        return pltpu.make_async_remote_copy(
            src_ref=src.at[c], dst_ref=dst.at[c], send_sem=send.at[c], recv_sem=recv.at[c],
            device_id={"tensor": other}, device_id_type=MESH,
        )

    copy_a = lambda c: hand(part_a, got_a, send_a, recv_a, c, near)
    copy_b = lambda c: hand(part_b, got_b, send_b, recv_b, c, far)
    copy_c = lambda c: hand(part_c, got_c, send_c, recv_c, c, near)

    @pl.loop(0, chunks)
    def _(c):
        part_a[c] = share(flip(me, 3), c).astype(jnp.bfloat16)
        copy_a(c).start()

    @pl.loop(0, chunks)
    def _(c):
        own = share(far, c)
        copy_a(c).wait_recv()
        part_b[c] = (own + got_a[c].astype(jnp.float32)).astype(jnp.bfloat16)
        copy_b(c).start()

    @pl.loop(0, chunks)
    def _(c):
        part_c[c] = share(near, c).astype(jnp.bfloat16)
        copy_c(c).start()

    @pl.loop(0, chunks)
    def _(c):
        columns = pl.ds(pl.multiple_of(c * wide, wide), wide)
        total = share(me, c) + mine[:, columns].astype(jnp.float32)
        copy_c(c).wait_recv()
        total = total + got_c[c].astype(jnp.float32)
        copy_b(c).wait_recv()
        out_ref[:, columns] = (total + got_b[c].astype(jnp.float32)).astype(jnp.bfloat16)

    @pl.loop(0, chunks)
    def _(c):
        copy_a(c).wait_send()
        copy_b(c).wait_send()
        copy_c(c).wait_send()


def attend_call(q, kv, starts, tokens, w_out, dp):
    heads, count, _ = q.shape
    rows, width = tokens.shape
    reach = min(dp // 2 + 1, dp - 1)
    slots = reach + 2
    chunks = 8
    any_spec = pl.BlockSpec(memory_space=pl.ANY)
    vmem = pl.BlockSpec(memory_space=pltpu.VMEM)
    pieces = pltpu.VMEM((chunks, rows, width // chunks), jnp.bfloat16)
    sems = pltpu.SemaphoreType.DMA((chunks,))
    return pl.pallas_call(
        functools.partial(attend_kernel, dp, reach, chunks),
        out_shape=jax.ShapeDtypeStruct((rows, width), jnp.bfloat16),
        in_specs=[vmem, vmem, vmem, any_spec, any_spec],
        out_specs=vmem,
        scratch_shapes=[
            pltpu.VMEM((slots, 2, count, HEAD_SIZE), jnp.bfloat16),
            pltpu.VMEM((heads, count, 1), jnp.float32),
            pltpu.VMEM((heads, count, 1), jnp.float32),
            pltpu.VMEM((heads, count, HEAD_SIZE), jnp.float32),
            pltpu.VMEM((count, heads * HEAD_SIZE), jnp.bfloat16),
            pltpu.VMEM(w_out.shape, jnp.bfloat16),
            pieces, pieces, pieces, pieces, pieces, pieces,
            pltpu.VMEM((rows, width), jnp.bfloat16),
            pltpu.SemaphoreType.DMA((2,)),
            pltpu.SemaphoreType.DMA((slots,)),
            pltpu.SemaphoreType.DMA((slots,)),
            pltpu.SemaphoreType.DMA((slots,)),
            sems, sems, sems, sems, sems, sems,
        ],
        compiler_params=pltpu.CompilerParams(
            collective_id=1, has_side_effects=True, vmem_limit_bytes=60 * 2**20
        ),
        name="attend_scatter",
    )(q, kv, starts, tokens, w_out)


def body(tokens, norm_gain, w_query, key_weight, value_weight, w_out, lengths):
    tensor = lax.axis_size("tensor")
    dp = lax.axis_size("dp")
    count = tokens.shape[0] * tensor
    positions = lax.axis_index("dp") * count + jnp.arange(count, dtype=jnp.int32)
    starts = doc_starts(lengths, positions)
    half = HEAD_SIZE // 2
    exponent = jnp.arange(half, dtype=jnp.float32) * (-2.0 / HEAD_SIZE)
    angles = (positions - starts).astype(jnp.float32)[:, None] * (rope_base**exponent)[None, :]
    cos, sin = jnp.cos(angles), jnp.sin(angles)
    cos = jnp.concatenate([cos, cos], axis=1)
    sin = jnp.concatenate([-sin, sin], axis=1)
    q, kv = project_call(
        tokens, norm_gain[None, :], cos, sin, w_query, key_weight, value_weight, tensor
    )
    return attend_call(q, kv, starts[:, None], tokens, w_out, dp)


def solution(mesh):
    in_specs = (
        P(("dp", "tensor"), None),
        P(),
        P(None, "tensor"),
        P(None, "tensor"),
        P(None, "tensor"),
        P("tensor", None),
        P(),
    )
    out_specs = P(("dp", "tensor"), None)
    return jax.shard_map(body, mesh=mesh, in_specs=in_specs, out_specs=out_specs, check_vma=False)
```

time: 205 us -> 107 us (0.52)
  the two profiles are of different devices: /device:TPU:0 before, /device:TPU:24 now
where the time goes in v1:
time: 107 us
  Pallas kernels  100 us (93%)
  other arithmetic  3.57 us (3%)
  local copies, waits for them, and re-layouts  3.15 us (3%)
    pallas_call x1, Pallas kernels, attend_call(): pl.pallas_call(functools.partial(attend_kernel, dp, reach, chunks), out_s...  68.2 us
    pallas_call x1, Pallas kernels, project_call(): pl.pallas_call(functools.partial(project_kernel, chunks), out_shape=(jax....  32.1 us
    unnamed x1, local copies, waits for them, and re-layouts  2.29 us

profile of v1, /device:TPU:24, one launch (start us, length us, event | category | flops | bytes accessed | tf_op | source)
XLA Modules:
  0.0 107.0 jit_solution(10933283709156135881)
XLA Ops:
  0.0 0.8 reduce-window.8
  0.8 0.7 select_reduce_fusion
  1.6 0.9 copy.9.starts
  2.5 1.0 fusion
  3.4 1.0 pad_maximum_fusion
  4.4 32.1 %gather_project.1 = (bf16[4,512,128]{2,1,0:T(8,128)(2,1)}, bf16[2,512,128]{2,1,0:T(8,128)(2,1)}) custom-call(bf16[128,4096]{1,0:T(8,128)(2,1)} %tokens.3, f32[1,4096]{1,0:T(1,128)} %bitcast.5, f32[512,128]{1,0:T(8,128)} %get-tuple-element.12.cos_ref, f32[512,128]{1,0:T(8,128)} %get-tuple-element.13.sin_ref, bf16[4096,512]{1,0:T(8,128)(2,1)} %wq.1, ...), custom_call_target="tpu_custom_call" | custom-call | tf_op jit(solution)/shard_map/gather_project/pallas_call | solution.py:134
  36.5 68.2 %attend_scatter.1 = bf16[128,4096]{1,0:T(8,128)(2,1)} custom-call(bf16[4,512,128]{2,1,0:T(8,128)(2,1)} %get-tuple-element.7.q_ref, bf16[2,512,128]{2,1,0:T(8,128)(2,1)} %get-tuple-element.8.kv_ref, s32[512,1]{1,0:T(8,128)} %copy.9.starts, bf16[128,4096]{1,0:T(8,128)(2,1)} %tokens.3, bf16[512,4096]{1,0:T(8,128)(2,1)} %w_out.1), custom_call_target="tpu_custom_call" | custom-call | tf_op jit(solution)/shard_map/attend_scatter/pallas_call | solution.py:378
  104.7 2.3 %copy.11 = bf16[128,4096]{1,0:T(8,128)(2,1)} copy(bf16[128,4096]{1,0:T(8,128)(2,1)} %attend_scatter.1) | data formatting | bytes 2097152
  (3 shorter events, 0.0 us)

commit v2 on v0

v2 whole, which is shorter than its diff:
```python
import functools
import math

import jax
import jax.numpy as jnp
from jax import lax
from jax.experimental import pallas as pl
from jax.experimental.pallas import tpu as pltpu
from jax.sharding import PartitionSpec as P

HEAD_SIZE = 128
MESH = pl.DeviceIdType.MESH

epsilon = 1e-05
rope_base = 500000.0
masked = -1e30


def flip(index, bits):
    low, high = index % 2, index // 2
    if bits & 1:
        low = 1 - low
    if bits & 2:
        high = 1 - high
    return high * 2 + low


def kernel(
    dp, reach, pieces, chunks,
    lengths, gain, frequency, tokens, wq, wk, wv, w_out,
    out_ref,
    held, normed, weight, raw, cos_ref, sin_ref, query, keys, peak, mass, summed, attended, weight_out,
    part_a, part_b, part_c, got_a, got_b, got_c,
    load_sem, send1, recv1, send2, recv2, send3, recv3, z_send, x_send, ring_recv,
    send_a, recv_a, send_b, recv_b, send_c, recv_c,
):
    me = lax.axis_index("tensor")
    here = lax.axis_index("dp")
    odd = here % 2
    partner = here + 1 - 2 * odd
    near, far = flip(me, 1), flip(me, 2)
    rows = tokens.shape[0]
    count = 4 * rows
    half = 2 * rows
    heads = query.shape[0]
    lanes = HEAD_SIZE
    q_width, kv_width = wq.shape[1], wk.shape[1]
    last_even = reach + 1 if reach % 2 else reach

    loads = [
        pltpu.make_async_copy(tokens, held.at[0], load_sem.at[0]),
        pltpu.make_async_copy(wq, weight.at[:, pl.ds(0, q_width)], load_sem.at[1]),
        pltpu.make_async_copy(wk, weight.at[:, pl.ds(q_width, kv_width)], load_sem.at[2]),
        pltpu.make_async_copy(wv, weight.at[:, pl.ds(q_width + kv_width, kv_width)], load_sem.at[3]),
    ]
    load_out = pltpu.make_async_copy(w_out, weight_out, load_sem.at[4])

    barrier = pltpu.get_barrier_semaphore()
    for other in (near, far):
        pl.semaphore_signal(barrier, inc=1, device_id={"tensor": other}, device_id_type=MESH)
    for other in (partner, (here + 2) % dp, (here + dp - 2) % dp):
        pl.semaphore_signal(barrier, inc=1, device_id={"dp": other}, device_id_type=MESH)
    for load in loads:
        load.start()
    pl.semaphore_wait(barrier, 5)

    def remote(src, dst, send, recv, axis, other):
        return pltpu.make_async_remote_copy(
            src_ref=src, dst_ref=dst, send_sem=send, recv_sem=recv,
            device_id={axis: other}, device_id_type=MESH,
        )

    piece = rows // pieces
    cross, relays = [], []
    for c in range(pieces):
        span = pl.ds(c * piece, piece)
        cross.append(remote(tokens.at[span, :], held.at[2, span, :], send2.at[c], recv2.at[c], "tensor", far))
        relays.append(remote(held.at[2, span, :], held.at[3, span, :], send3.at[c], recv3.at[c], "tensor", near))
    for copy in cross:
        copy.start()
    sideways = remote(tokens, held.at[1], send1, recv1, "tensor", near)
    sideways.start()
    load_out.start()

    lane = lax.broadcasted_iota(jnp.int32, (1, lanes), 1)
    begin = jnp.zeros((1, lanes), jnp.int32)
    end = jnp.zeros((1, lanes), jnp.int32)
    total = jnp.int32(0)
    for e in range(lengths.shape[0]):
        begin = jnp.where(lane == e, total, begin)
        total = total + lengths[e]
        end = jnp.where(lane == e, total, end)
    sign = jnp.where(lane < lanes // 2, -1.0, 1.0)

    def inside(first, number):
        position = first + lax.broadcasted_iota(jnp.int32, (number, 1), 0)
        return position, (position >= begin) & (position < end)

    @pl.loop(0, 4)
    def _(b):
        first = pl.multiple_of(b * rows, rows)
        position, belongs = inside(here * count + first, rows)
        start = jnp.sum(jnp.where(belongs, begin.astype(jnp.float32), 0.0), axis=1, keepdims=True)
        angle = (position.astype(jnp.float32) - start) * frequency[...]
        cos_ref[pl.ds(first, rows), :] = jnp.cos(angle)
        sin_ref[pl.ds(first, rows), :] = jnp.sin(angle) * sign
        mark = jnp.where(belongs, 1.0, 0.0).astype(jnp.bfloat16)
        for h in range(heads):
            query[h, pl.ds(first, rows), 0:lanes] = mark

    for h in range(2):
        pair = me // 2 if h == 0 else 1 - me // 2

        @pl.loop(0, reach + 1)
        def _(j):
            slot = pl.ds(pl.multiple_of(j * half, half), half)
            _, belongs = inside((here - j) * count + pair * half, half)
            keys[h, slot, 0:lanes] = jnp.where(belongs, 0.0, masked).astype(jnp.bfloat16)

            @pl.when(here < j)
            def _():
                keys[h, slot, lanes:3 * lanes] = jnp.zeros((half, 2 * lanes), jnp.bfloat16)

    def part(j, h):
        return keys.at[h, pl.ds(pl.multiple_of(j * half, half), half), pl.ds(lanes, 2 * lanes)]

    def along(j, h):
        return remote(part(j, h), part(j + 2, h), z_send.at[j, h], ring_recv.at[j + 2, h], "dp", here + 2)

    def across(j, h):
        target = j + 1 - 2 * odd
        return remote(part(j, h), part(target, h), x_send.at[j, h], ring_recv.at[target, h], "dp", partner)

    def goes_along(j):
        return (here + 2 < dp) & (j + 2 <= reach + odd) & (here >= j)

    def goes_across(j):
        target = j + 1 - 2 * odd
        return (target >= 1) & (target <= reach) & (here >= j)

    def forward(j, h):
        @pl.when(goes_along(j))
        def _():
            along(j, h).start()

        @pl.when(goes_across(j))
        def _():
            across(j, h).start()

    def settle(j, h):
        @pl.when(goes_along(j))
        def _():
            along(j, h).wait_send()

        @pl.when(goes_across(j))
        def _():
            across(j, h).wait_send()

    def arrive(j, h):
        remote(part(j, h), part(j, h), z_send.at[j, h], ring_recv.at[j, h], "dp", partner).wait_recv()

    def pass_on(j, h):
        @pl.when((here >= j) & (j <= reach + odd))
        def _():
            arrive(j, h)
            forward(j, h)

    def odd_arrivals(h):
        for j in range(1, reach + 1, 2):
            @pl.when(here >= j)
            def _():
                arrive(j, h)

    def project(slot):
        block = flip(me, slot)
        first = pl.multiple_of(block * rows, rows)
        wide = held[slot].astype(jnp.float32)
        inverse = lax.rsqrt(jnp.mean(wide * wide, axis=1, keepdims=True) + epsilon)
        normed[...] = (wide * inverse * gain[...]).astype(jnp.bfloat16)
        tile = 256

        @pl.loop(0, weight.shape[1] // tile)
        def _(n):
            columns = pl.ds(pl.multiple_of(n * tile, tile), tile)
            raw[:, columns] = jnp.dot(normed[...], weight[:, columns], preferred_element_type=jnp.float32)

        cos = cos_ref[pl.ds(first, rows), :]
        sin = sin_ref[pl.ds(first, rows), :]

        def rotated(index):
            entry = raw[:, index * lanes:(index + 1) * lanes]
            return (entry * cos + pltpu.roll(entry, lanes // 2, 1) * sin).astype(jnp.bfloat16)

        for h in range(heads):
            query[h, pl.ds(first, rows), lanes:2 * lanes] = rotated(h)
        place = pl.ds(pl.multiple_of(block % 2 * rows, rows), rows)
        keys[slot // 2, place, lanes:2 * lanes] = rotated(heads)
        keys[slot // 2, place, 2 * lanes:3 * lanes] = raw[:, (heads + 1) * lanes:].astype(jnp.bfloat16)

    scale = HEAD_SIZE ** (-0.5) * math.log2(math.e)
    seen = (reach + 1) * half

    def fold(slot, h, opening):
        first = pl.multiple_of(flip(me, slot) * rows, rows)
        span = pl.ds(first, rows)
        pair = me // 2 if h == 0 else 1 - me // 2
        key_pos = pair * half + lax.broadcasted_iota(jnp.int32, (rows, half), 1)
        query_pos = first + lax.broadcasted_iota(jnp.int32, (rows, 1), 0)
        causal = key_pos <= query_pos

        def one(g):
            scores = lax.dot_general(
                query[g, span, :], keys[h, 0:seen, 0:2 * lanes], (((1,), (1,)), ((), ())),
                preferred_element_type=jnp.float32,
            )
            scores = jnp.concatenate(
                [jnp.where(causal, scores[:, :half], masked), scores[:, half:]], axis=1
            )
            top = jnp.max(scores, axis=1, keepdims=True)
            if not opening:
                old = peak[g, span, :]
                top = jnp.maximum(old, top)
            else:
                top = jnp.maximum(top, -1e29)
            probs = jnp.exp2(scores * scale - top * scale)
            added = jnp.sum(probs, axis=1, keepdims=True)
            update = jnp.dot(
                probs.astype(jnp.bfloat16), keys[h, 0:seen, 2 * lanes:3 * lanes],
                preferred_element_type=jnp.float32,
            )
            if opening:
                peak[g, span, :] = top
                mass[g, span, :] = added
                summed[g, span, :] = update
            else:
                shrink = jnp.exp2((old - top) * scale)
                whole = mass[g, span, :] * shrink + added
                result = (summed[g, span, :] * shrink + update) / whole
                attended[g, span, :] = result.astype(jnp.bfloat16)

        @pl.loop(0, heads // 2)
        def _(i):
            one(2 * i)
            one(2 * i + 1)

    for load in loads:
        load.wait()
    project(0)
    sideways.wait_recv()
    project(1)
    forward(0, 0)
    hops = list(range(2, last_even + 1, 2))
    for c in range(pieces):
        cross[c].wait_recv()
        relays[c].start()
        share_of = hops[len(hops) * c // pieces:len(hops) * (c + 1) // pieces]
        for j in share_of:
            pass_on(j, 0)
    project(2)
    for relay in relays:
        relay.wait_recv()
    project(3)
    forward(0, 1)

    odd_arrivals(0)
    order = (0, 1, 2, 3)
    for n in range(4):
        fold(order[n], 0, True)
        for j in hops[len(hops) * n // 4:len(hops) * (n + 1) // 4]:
            pass_on(j, 1)
    odd_arrivals(1)

    load_out.wait()
    wide = weight_out.shape[1] // chunks

    def share(block_of, c):
        first = pl.multiple_of(block_of * rows, rows)
        columns = pl.ds(pl.multiple_of(c * wide, wide), wide)
        joined = jnp.concatenate([attended[g, pl.ds(first, rows), :] for g in range(heads)], axis=1)
        return jnp.dot(joined, weight_out[:, columns], preferred_element_type=jnp.float32)

    def hand(src, dst, send, recv, c, other):
        return remote(src.at[c], dst.at[c], send.at[c], recv.at[c], "tensor", other)

    copy_a = lambda c: hand(part_a, got_a, send_a, recv_a, c, near)
    copy_b = lambda c: hand(part_b, got_b, send_b, recv_b, c, far)
    copy_c = lambda c: hand(part_c, got_c, send_c, recv_c, c, near)

    fold(3, 1, False)

    @pl.loop(0, chunks)
    def _(c):
        part_a[c] = share(flip(me, 3), c).astype(jnp.bfloat16)
        copy_a(c).start()

    fold(2, 1, False)

    @pl.loop(0, chunks)
    def _(c):
        own = share(far, c)
        copy_a(c).wait_recv()
        part_b[c] = (own + got_a[c].astype(jnp.float32)).astype(jnp.bfloat16)
        copy_b(c).start()

    fold(1, 1, False)

    @pl.loop(0, chunks)
    def _(c):
        part_c[c] = share(near, c).astype(jnp.bfloat16)
        copy_c(c).start()

    fold(0, 1, False)

    @pl.loop(0, chunks)
    def _(c):
        columns = pl.ds(pl.multiple_of(c * wide, wide), wide)
        result = share(me, c) + held[0, :, columns].astype(jnp.float32)
        copy_c(c).wait_recv()
        result = result + got_c[c].astype(jnp.float32)
        copy_b(c).wait_recv()
        out_ref[:, columns] = (result + got_b[c].astype(jnp.float32)).astype(jnp.bfloat16)

    @pl.loop(0, chunks)
    def _(c):
        copy_a(c).wait_send()
        copy_b(c).wait_send()
        copy_c(c).wait_send()

    sideways.wait_send()
    for copy in cross + relays:
        copy.wait_send()
    for h in range(2):
        for j in range(0, last_even + 1, 2):
            @pl.when(j <= reach + odd)
            def _():
                settle(j, h)


def body(tokens, norm_gain, w_query, key_weight, value_weight, w_out, lengths):
    dp = lax.axis_size("dp")
    rows, width = tokens.shape
    count = 4 * rows
    heads = w_query.shape[1] // HEAD_SIZE
    total = w_query.shape[1] + key_weight.shape[1] + value_weight.shape[1]
    reach = min(dp // 2 + 1, dp - 1)
    slots = reach + 2
    pieces, chunks = 4, 8
    exponent = jnp.arange(HEAD_SIZE // 2, dtype=jnp.float32) * (-2.0 / HEAD_SIZE)
    frequency = jnp.tile(rope_base**exponent, 2)[None, :]
    any_spec = pl.BlockSpec(memory_space=pl.ANY)
    vmem = pl.BlockSpec(memory_space=pltpu.VMEM)
    smem = pl.BlockSpec(memory_space=pltpu.SMEM)
    bf16, f32 = jnp.bfloat16, jnp.float32
    part = pltpu.VMEM((chunks, rows, width // chunks), bf16)
    dma = pltpu.SemaphoreType.DMA
    return pl.pallas_call(
        functools.partial(kernel, dp, reach, pieces, chunks),
        out_shape=jax.ShapeDtypeStruct((rows, width), bf16),
        in_specs=[smem, vmem, vmem, any_spec, any_spec, any_spec, any_spec, any_spec],
        out_specs=vmem,
        scratch_shapes=[
            pltpu.VMEM((4, rows, width), bf16),
            pltpu.VMEM((rows, width), bf16),
            pltpu.VMEM((width, total), bf16),
            pltpu.VMEM((rows, total), f32),
            pltpu.VMEM((count, HEAD_SIZE), f32),
            pltpu.VMEM((count, HEAD_SIZE), f32),
            pltpu.VMEM((heads, count, 2 * HEAD_SIZE), bf16),
            pltpu.VMEM((2, slots * 2 * rows, 3 * HEAD_SIZE), bf16),
            pltpu.VMEM((heads, count, 1), f32),
            pltpu.VMEM((heads, count, 1), f32),
            pltpu.VMEM((heads, count, HEAD_SIZE), f32),
            pltpu.VMEM((heads, count, HEAD_SIZE), bf16),
            pltpu.VMEM(w_out.shape, bf16),
            part, part, part, part, part, part,
            dma((5,)), dma, dma,
            dma((pieces,)), dma((pieces,)), dma((pieces,)), dma((pieces,)),
            dma((slots, 2)), dma((slots, 2)), dma((slots, 2)),
            dma((chunks,)), dma((chunks,)), dma((chunks,)), dma((chunks,)), dma((chunks,)), dma((chunks,)),
        ],
        compiler_params=pltpu.CompilerParams(
            collective_id=0, has_side_effects=True, vmem_limit_bytes=62 * 2**20
        ),
        name="attention_block",
    )(lengths, norm_gain[None, :], frequency, tokens, w_query, key_weight, value_weight, w_out)


def solution(mesh):
    in_specs = (
        P(("dp", "tensor"), None),
        P(),
        P(None, "tensor"),
        P(None, "tensor"),
        P(None, "tensor"),
        P("tensor", None),
        P(),
    )
    out_specs = P(("dp", "tensor"), None)
    return jax.shard_map(body, mesh=mesh, in_specs=in_specs, out_specs=out_specs, check_vma=False)
```

time: 205 us -> 83 us (0.40)
  the two profiles are of different devices: /device:TPU:0 before, /device:TPU:24 now
where the time goes in v2:
time: 83 us; the launch traced here: 82.8 us
  Pallas kernels  79.9 us (96%)
  local copies, waits for them, and re-layouts  2.89 us (3%)
    pallas_call x1, Pallas kernels, body(): pl.pallas_call(functools.partial(kernel, dp, reach, pieces, chunks), out_...  79.9 us
    unnamed x1, local copies, waits for them, and re-layouts  2.29 us

profile of v2, /device:TPU:24, one launch (start us, length us, event | category | flops | bytes accessed | tf_op | source)
XLA Modules:
  0.0 82.8 jit_solution(3803319993225931587)
XLA Ops:
  0.0 0.6 broadcast_in_dim_tile.3.frequency
  0.6 79.9 %attention_block.1 = bf16[128,4096]{1,0:T(8,128)(2,1)} custom-call(s32[4]{0:T(128)} %lengths.1, f32[1,4096]{1,0:T(1,128)} %bitcast.1, f32[1,128]{1,0:T(1,128)} %broadcast_in_dim_tile.3.frequency, bf16[128,4096]{1,0:T(8,128)(2,1)} %tokens.1, bf16[4096,512]{1,0:T(8,128)(2,1)} %wq.1, bf16[4096,128]{1,0:T(8,128)(2,1)} %wk.1, bf16[4096,128]{1,0:T(8,128)(2,1)} %wv.1, ...), custom_call_target="tpu_custom_call" | custom-call | tf_op jit(solution)/shard_map/attention_block/pallas_call | solution.py:356
  80.5 2.3 %copy.9 = bf16[128,4096]{1,0:T(8,128)(2,1)} copy(bf16[128,4096]{1,0:T(8,128)(2,1)} %attention_block.1) | data formatting | bytes 2097152
  (2 shorter events, 0.0 us)

commit v3 on v2

--- a/solution.py
+++ b/solution.py
@@ -29,9 +29,9 @@
     dp, reach, pieces, chunks,
     lengths, gain, frequency, tokens, wq, wk, wv, w_out,
     out_ref,
-    held, normed, weight, raw, cos_ref, sin_ref, query, keys, peak, mass, summed, attended, weight_out,
+    held, normed, weight, raw, cos_ref, sin_ref, query, keys_near, keys_first, keys_last, peak, mass, summed, attended, weight_out,
     part_a, part_b, part_c, got_a, got_b, got_c,
-    load_sem, send1, recv1, send2, recv2, send3, recv3, z_send, x_send, ring_recv,
+    load_sem, send1, recv1, send2, recv2, send3, recv3, z_send, x_send, d_send, ring_recv,
     send_a, recv_a, send_b, recv_b, send_c, recv_c,
 ):
     me = lax.axis_index("tensor")
@@ -41,11 +41,13 @@
     near, far = flip(me, 1), flip(me, 2)
     rows = tokens.shape[0]
     count = 4 * rows
-    half = 2 * rows
     heads = query.shape[0]
     lanes = HEAD_SIZE
     q_width, kv_width = wq.shape[1], wk.shape[1]
-    last_even = reach + 1 if reach % 2 else reach
+    last_even = reach - reach % 2
+    groups = (keys_near, keys_first, keys_last)
+    sizes = (2 * rows, rows, rows)
+    batch = rows // 2
 
     loads = [
         pltpu.make_async_copy(tokens, held.at[0], load_sem.at[0]),
@@ -58,11 +60,12 @@
     barrier = pltpu.get_barrier_semaphore()
     for other in (near, far):
         pl.semaphore_signal(barrier, inc=1, device_id={"tensor": other}, device_id_type=MESH)
-    for other in (partner, (here + 2) % dp, (here + dp - 2) % dp):
+    ways = (partner, (here + 2) % dp, (here + dp - 2) % dp, (here + reach) % dp, (here + dp - reach) % dp)
+    for other in ways:
         pl.semaphore_signal(barrier, inc=1, device_id={"dp": other}, device_id_type=MESH)
     for load in loads:
         load.start()
-    pl.semaphore_wait(barrier, 5)
+    pl.semaphore_wait(barrier, 7)
 
     def remote(src, dst, send, recv, axis, other):
         return pltpu.make_async_remote_copy(
@@ -92,14 +95,13 @@
         end = jnp.where(lane == e, total, end)
     sign = jnp.where(lane < lanes // 2, -1.0, 1.0)
 
-    def inside(first, number):
-        position = first + lax.broadcasted_iota(jnp.int32, (number, 1), 0)
+    def inside(position):
         return position, (position >= begin) & (position < end)
 
     @pl.loop(0, 4)
     def _(b):
         first = pl.multiple_of(b * rows, rows)
-        position, belongs = inside(here * count + first, rows)
+        position, belongs = inside(here * count + first + lax.broadcasted_iota(jnp.int32, (rows, 1), 0))
         start = jnp.sum(jnp.where(belongs, begin.astype(jnp.float32), 0.0), axis=1, keepdims=True)
         angle = (position.astype(jnp.float32) - start) * frequency[...]
         cos_ref[pl.ds(first, rows), :] = jnp.cos(angle)
@@ -108,21 +110,29 @@
         for h in range(heads):
             query[h, pl.ds(first, rows), 0:lanes] = mark
 
-    for h in range(2):
-        pair = me // 2 if h == 0 else 1 - me // 2
+    def places(h, index):
+        if h == 0:
+            return me // 2 * (2 * rows) + index
+        skip = (h - 1) * batch
+        return index + skip + jnp.where(index < batch, far * rows, flip(me, 3) * rows - batch)
+
+    for h in range(3):
+        size = sizes[h]
 
         @pl.loop(0, reach + 1)
         def _(j):
-            slot = pl.ds(pl.multiple_of(j * half, half), half)
-            _, belongs = inside((here - j) * count + pair * half, half)
-            keys[h, slot, 0:lanes] = jnp.where(belongs, 0.0, masked).astype(jnp.bfloat16)
+            slot = pl.ds(pl.multiple_of(j * size, size), size)
+            place = places(h, lax.broadcasted_iota(jnp.int32, (size, 1), 0))
+            _, belongs = inside((here - j) * count + place)
+            groups[h][slot, 0:lanes] = jnp.where(belongs, 0.0, masked).astype(jnp.bfloat16)
 
             @pl.when(here < j)
             def _():
-                keys[h, slot, lanes:3 * lanes] = jnp.zeros((half, 2 * lanes), jnp.bfloat16)
+                groups[h][slot, lanes:3 * lanes] = jnp.zeros((size, 2 * lanes), jnp.bfloat16)
 
     def part(j, h):
-        return keys.at[h, pl.ds(pl.multiple_of(j * half, half), half), pl.ds(lanes, 2 * lanes)]
+        size = sizes[h]
+        return groups[h].at[pl.ds(pl.multiple_of(j * size, size), size), pl.ds(lanes, 2 * lanes)]
 
     def along(j, h):
         return remote(part(j, h), part(j + 2, h), z_send.at[j, h], ring_recv.at[j + 2, h], "dp", here + 2)
@@ -131,26 +141,44 @@
         target = j + 1 - 2 * odd
         return remote(part(j, h), part(target, h), x_send.at[j, h], ring_recv.at[target, h], "dp", partner)
 
+    direct_used = reach % 2 == 1
+    goes_direct = (odd == 1) & (here + reach < dp)
+
+    def direct(h):
+        return remote(part(0, h), part(reach, h), d_send.at[h], ring_recv.at[reach, h], "dp", here + reach)
+
     def goes_along(j):
-        return (here + 2 < dp) & (j + 2 <= reach + odd) & (here >= j)
+        return (here + 2 < dp) & (here >= j)
 
     def goes_across(j):
         target = j + 1 - 2 * odd
         return (target >= 1) & (target <= reach) & (here >= j)
 
     def forward(j, h):
-        @pl.when(goes_along(j))
-        def _():
-            along(j, h).start()
+        if j == 0 and direct_used:
+            @pl.when(goes_direct)
+            def _():
+                direct(h).start()
+
+        if j + 2 <= reach:
+            @pl.when(goes_along(j))
+            def _():
+                along(j, h).start()
 
         @pl.when(goes_across(j))
         def _():
             across(j, h).start()
 
     def settle(j, h):
-        @pl.when(goes_along(j))
-        def _():
-            along(j, h).wait_send()
+        if j == 0 and direct_used:
+            @pl.when(goes_direct)
+            def _():
+                direct(h).wait_send()
+
+        if j + 2 <= reach:
+            @pl.when(goes_along(j))
+            def _():
+                along(j, h).wait_send()
 
         @pl.when(goes_across(j))
         def _():
@@ -160,7 +188,7 @@
         remote(part(j, h), part(j, h), z_send.at[j, h], ring_recv.at[j, h], "dp", partner).wait_recv()
 
     def pass_on(j, h):
-        @pl.when((here >= j) & (j <= reach + odd))
+        @pl.when(here >= j)
         def _():
             arrive(j, h)
             forward(j, h)
@@ -171,12 +199,13 @@
             def _():
                 arrive(j, h)
 
-    def project(slot):
-        block = flip(me, slot)
-        first = pl.multiple_of(block * rows, rows)
-        wide = held[slot].astype(jnp.float32)
-        inverse = lax.rsqrt(jnp.mean(wide * wide, axis=1, keepdims=True) + epsilon)
-        normed[...] = (wide * inverse * gain[...]).astype(jnp.bfloat16)
+    def project(h, parts):
+        row = 0
+        for slot, skip, number in parts:
+            rows_of = held[slot, skip:skip + number, :].astype(jnp.float32)
+            inverse = lax.rsqrt(jnp.mean(rows_of * rows_of, axis=1, keepdims=True) + epsilon)
+            normed[row:row + number, :] = (rows_of * inverse * gain[...]).astype(jnp.bfloat16)
+            row += number
         tile = 256
 
         @pl.loop(0, weight.shape[1] // tile)
@@ -184,37 +213,41 @@
             columns = pl.ds(pl.multiple_of(n * tile, tile), tile)
             raw[:, columns] = jnp.dot(normed[...], weight[:, columns], preferred_element_type=jnp.float32)
 
-        cos = cos_ref[pl.ds(first, rows), :]
-        sin = sin_ref[pl.ds(first, rows), :]
-
-        def rotated(index):
-            entry = raw[:, index * lanes:(index + 1) * lanes]
-            return (entry * cos + pltpu.roll(entry, lanes // 2, 1) * sin).astype(jnp.bfloat16)
-
-        for h in range(heads):
-            query[h, pl.ds(first, rows), lanes:2 * lanes] = rotated(h)
-        place = pl.ds(pl.multiple_of(block % 2 * rows, rows), rows)
-        keys[slot // 2, place, lanes:2 * lanes] = rotated(heads)
-        keys[slot // 2, place, 2 * lanes:3 * lanes] = raw[:, (heads + 1) * lanes:].astype(jnp.bfloat16)
+        row = 0
+        for slot, skip, number in parts:
+            block = flip(me, slot)
+            here_rows = pl.ds(pl.multiple_of(block * rows + skip, number), number)
+            cos, sin = cos_ref[here_rows, :], sin_ref[here_rows, :]
+
+            def rotated(index):
+                entry = raw[row:row + number, index * lanes:(index + 1) * lanes]
+                return (entry * cos + pltpu.roll(entry, lanes // 2, 1) * sin).astype(jnp.bfloat16)
+
+            for g in range(heads):
+                query[g, here_rows, lanes:2 * lanes] = rotated(g)
+            place = pl.ds(pl.multiple_of(block % 2 * rows, rows), rows) if h == 0 else pl.ds(row, number)
+            groups[h][place, lanes:2 * lanes] = rotated(heads)
+            groups[h][place, 2 * lanes:3 * lanes] = raw[row:row + number, (heads + 1) * lanes:].astype(jnp.bfloat16)
+            row += number
 
     scale = HEAD_SIZE ** (-0.5) * math.log2(math.e)
-    seen = (reach + 1) * half
-
-    def fold(slot, h, opening):
+
+    def fold(slot, h, opening=False, closing=False):
+        size = sizes[h]
+        store = groups[h]
         first = pl.multiple_of(flip(me, slot) * rows, rows)
         span = pl.ds(first, rows)
-        pair = me // 2 if h == 0 else 1 - me // 2
-        key_pos = pair * half + lax.broadcasted_iota(jnp.int32, (rows, half), 1)
+        key_pos = places(h, lax.broadcasted_iota(jnp.int32, (rows, size), 1))
         query_pos = first + lax.broadcasted_iota(jnp.int32, (rows, 1), 0)
         causal = key_pos <= query_pos
 
         def one(g):
             scores = lax.dot_general(
-                query[g, span, :], keys[h, 0:seen, 0:2 * lanes], (((1,), (1,)), ((), ())),
+                query[g, span, :], store[:, 0:2 * lanes], (((1,), (1,)), ((), ())),
                 preferred_element_type=jnp.float32,
             )
             scores = jnp.concatenate(
-                [jnp.where(causal, scores[:, :half], masked), scores[:, half:]], axis=1
+                [jnp.where(causal, scores[:, :size], masked), scores[:, size:]], axis=1
             )
             top = jnp.max(scores, axis=1, keepdims=True)
             if not opening:
@@ -225,7 +258,7 @@
             probs = jnp.exp2(scores * scale - top * scale)
             added = jnp.sum(probs, axis=1, keepdims=True)
             update = jnp.dot(
-                probs.astype(jnp.bfloat16), keys[h, 0:seen, 2 * lanes:3 * lanes],
+                probs.astype(jnp.bfloat16), store[:, 2 * lanes:3 * lanes],
                 preferred_element_type=jnp.float32,
             )
             if opening:
@@ -235,40 +268,64 @@
             else:
                 shrink = jnp.exp2((old - top) * scale)
                 whole = mass[g, span, :] * shrink + added
-                result = (summed[g, span, :] * shrink + update) / whole
-                attended[g, span, :] = result.astype(jnp.bfloat16)
+                result = summed[g, span, :] * shrink + update
+                if closing:
+                    attended[g, span, :] = (result / whole).astype(jnp.bfloat16)
+                else:
+                    peak[g, span, :] = top
+                    mass[g, span, :] = whole
+                    summed[g, span, :] = result
 
         @pl.loop(0, heads // 2)
         def _(i):
             one(2 * i)
             one(2 * i + 1)
 
+    hops = list(range(2, last_even + 1, 2))
+    near_hops, late_hops = hops[:len(hops) // 2], hops[len(hops) // 2:]
+
+    def pass_all(which, h):
+        for j in which:
+            pass_on(j, h)
+
+    def gathered(c):
+        cross[c].wait_recv()
+        relays[c].start()
+
     for load in loads:
         load.wait()
-    project(0)
+    project(0, [(0, 0, rows)])
     sideways.wait_recv()
-    project(1)
+    project(0, [(1, 0, rows)])
     forward(0, 0)
-    hops = list(range(2, last_even + 1, 2))
-    for c in range(pieces):
-        cross[c].wait_recv()
-        relays[c].start()
-        share_of = hops[len(hops) * c // pieces:len(hops) * (c + 1) // pieces]
-        for j in share_of:
-            pass_on(j, 0)
-    project(2)
-    for relay in relays:
-        relay.wait_recv()
-    project(3)
+    for c in range(pieces // 2):
+        gathered(c)
+    for c in range(pieces // 2):
+        relays[c].wait_recv()
+    project(1, [(2, 0, batch), (3, 0, batch)])
     forward(0, 1)
-
+    pass_all(hops, 0)
     odd_arrivals(0)
-    order = (0, 1, 2, 3)
-    for n in range(4):
-        fold(order[n], 0, True)
-        for j in hops[len(hops) * n // 4:len(hops) * (n + 1) // 4]:
-            pass_on(j, 1)
+    for c in range(pieces // 2, pieces):
+        if c == pieces // 2:
+            fold(0, 0, opening=True)
+        if c == pieces - 1:
+            pass_all(near_hops, 1)
+            fold(1, 0, opening=True)
+        gathered(c)
+    for c in range(pieces // 2, pieces):
+        relays[c].wait_recv()
+    project(2, [(2, batch, batch), (3, batch, batch)])
+    forward(0, 2)
+    pass_all(late_hops, 1)
+    fold(3, 0, opening=True)
+    pass_all(near_hops, 2)
     odd_arrivals(1)
+    fold(2, 0, opening=True)
+    pass_all(late_hops, 2)
+    fold(3, 1)
+    fold(2, 1)
+    odd_arrivals(2)
 
     load_out.wait()
     wide = weight_out.shape[1] // chunks
@@ -286,14 +343,14 @@
     copy_b = lambda c: hand(part_b, got_b, send_b, recv_b, c, far)
     copy_c = lambda c: hand(part_c, got_c, send_c, recv_c, c, near)
 
-    fold(3, 1, False)
+    fold(3, 2, closing=True)
 
     @pl.loop(0, chunks)
     def _(c):
         part_a[c] = share(flip(me, 3), c).astype(jnp.bfloat16)
         copy_a(c).start()
 
-    fold(2, 1, False)
+    fold(2, 2, closing=True)
 
     @pl.loop(0, chunks)
     def _(c):
@@ -302,14 +359,16 @@
         part_b[c] = (own + got_a[c].astype(jnp.float32)).astype(jnp.bfloat16)
         copy_b(c).start()
 
-    fold(1, 1, False)
+    fold(1, 1)
+    fold(1, 2, closing=True)
 
     @pl.loop(0, chunks)
     def _(c):
         part_c[c] = share(near, c).astype(jnp.bfloat16)
         copy_c(c).start()
 
-    fold(0, 1, False)
+    fold(0, 1)
+    fold(0, 2, closing=True)
 
     @pl.loop(0, chunks)
     def _(c):
@@ -329,11 +388,9 @@
     sideways.wait_send()
     for copy in cross + relays:
         copy.wait_send()
-    for h in range(2):
+    for h in range(3):
         for j in range(0, last_even + 1, 2):
-            @pl.when(j <= reach + odd)
-            def _():
-                settle(j, h)
+            settle(j, h)
 
 
 def body(tokens, norm_gain, w_query, key_weight, value_weight, w_out, lengths):
@@ -343,7 +400,7 @@
     heads = w_query.shape[1] // HEAD_SIZE
     total = w_query.shape[1] + key_weight.shape[1] + value_weight.shape[1]
     reach = min(dp // 2 + 1, dp - 1)
-    slots = reach + 2
+    slots = reach + 1
     pieces, chunks = 4, 8
     exponent = jnp.arange(HEAD_SIZE // 2, dtype=jnp.float32) * (-2.0 / HEAD_SIZE)
     frequency = jnp.tile(rope_base**exponent, 2)[None, :]
@@ -366,7 +423,9 @@
             pltpu.VMEM((count, HEAD_SIZE), f32),
             pltpu.VMEM((count, HEAD_SIZE), f32),
             pltpu.VMEM((heads, count, 2 * HEAD_SIZE), bf16),
-            pltpu.VMEM((2, slots * 2 * rows, 3 * HEAD_SIZE), bf16),
+            pltpu.VMEM((slots * 2 * rows, 3 * HEAD_SIZE), bf16),
+            pltpu.VMEM((slots * rows, 3 * HEAD_SIZE), bf16),
+            pltpu.VMEM((slots * rows, 3 * HEAD_SIZE), bf16),
             pltpu.VMEM((heads, count, 1), f32),
             pltpu.VMEM((heads, count, 1), f32),
             pltpu.VMEM((heads, count, HEAD_SIZE), f32),
@@ -375,7 +434,7 @@
             part, part, part, part, part, part,
             dma((5,)), dma, dma,
             dma((pieces,)), dma((pieces,)), dma((pieces,)), dma((pieces,)),
-            dma((slots, 2)), dma((slots, 2)), dma((slots, 2)),
+            dma((slots, 3)), dma((slots, 3)), dma((3,)), dma((slots, 3)),
             dma((chunks,)), dma((chunks,)), dma((chunks,)), dma((chunks,)), dma((chunks,)), dma((chunks,)),
         ],
         compiler_params=pltpu.CompilerParams(

time: 83 us -> 89.2 us (1.075); the launches traced: 82.8 us -> 87.5 us
  Pallas kernels: 79.9 us -> 84.5 us
    pallas_call x1, Pallas kernels: 79.9 us -> 84.5 us  [body(): pl.pallas_call(functools.partial(kernel, dp, reach, pieces, chunks), out_...]
where the time goes in v3:
time: 89.2 us; the launch traced here: 87.5 us
  Pallas kernels  84.5 us (95%)
  local copies, waits for them, and re-layouts  2.89 us (3%)
    pallas_call x1, Pallas kernels, body(): pl.pallas_call(functools.partial(kernel, dp, reach, pieces, chunks), out_...  84.5 us
    unnamed x1, local copies, waits for them, and re-layouts  2.29 us

profile of v3, /device:TPU:24, one launch (start us, length us, event | category | flops | bytes accessed | tf_op | source)
XLA Modules:
  0.0 87.5 jit_solution(14475684089791856418)
XLA Ops:
  0.0 0.6 broadcast_in_dim_tile.3.frequency
  0.6 84.5 %attention_block.1 = bf16[128,4096]{1,0:T(8,128)(2,1)} custom-call(s32[4]{0:T(128)} %lengths.1, f32[1,4096]{1,0:T(1,128)} %bitcast.1, f32[1,128]{1,0:T(1,128)} %broadcast_in_dim_tile.3.frequency, bf16[128,4096]{1,0:T(8,128)(2,1)} %tokens.1, bf16[4096,512]{1,0:T(8,128)(2,1)} %wq.1, bf16[4096,128]{1,0:T(8,128)(2,1)} %wk.1, bf16[4096,128]{1,0:T(8,128)(2,1)} %wv.1, ...), custom_call_target="tpu_custom_call" | custom-call | tf_op jit(solution)/shard_map/attention_block/pallas_call | solution.py:413
  85.2 2.3 %copy.9 = bf16[128,4096]{1,0:T(8,128)(2,1)} copy(bf16[128,4096]{1,0:T(8,128)(2,1)} %attention_block.1) | data formatting | bytes 2097152
  (2 shorter events, 0.0 us)
